TPU v7x, 32 devices: a whole 2x2x4 slice. The times are simulated.
32 devices in a mesh: band: 8 (over z, y), lev: 4 (over x, core).
Axes of the slice: x: 2, y: 2, z: 4, core: 2. Of those that a mesh axis runs over, the one named last changes fastest.
Arguments:
- grid_adjoint: float32 [1024, 64, 2048], P('band', 'lev'), may hold values from -6 to 6
- trajectory: float32 [1024, 64, 2048], P('band', 'lev'), may hold values from -3 to 3
- legendre_north: float32 [512, 512, 512], P(('band', 'lev')), may hold values from -0.25 to 0.25
- slot_wavenumber: int32 [512], replicated, may hold values from 0 to 511, each once
- spectral_state: float32 [512, 512, 2, 64], P(('band', 'lev')), may hold values from -6 to 6
- to_modes: float32 [64, 64], replicated, may hold values from -0.75 to 0.75
- from_modes: float32 [64, 64], replicated, may hold values from -0.75 to 0.75
- rates: float32 [64], replicated, may hold values from 0.1 to 10
Outputs:
- spectral_out: float32 [512, 512, 2, 64], P(('band', 'lev'))
- grid_out: float32 [1024, 64, 2048], P('band', 'lev')
Inputs may be any that keep to these rules, and one draw needn't show every extreme that they name: `slot_wavenumber`: each wavenumber stands in exactly one slot.
All inputs are finite; a program needn't handle non-finite values.
Results may differ from a plain program's by a relative error of at most 0.000067.
Values sent between devices are 32-bit elements; how exact they have to be, the bound alone decides.
A program may use at most 192 MiB of HBM per device.

v0:
```python
import jax
import jax.numpy as jnp
from jax import lax
from jax.sharding import PartitionSpec as P


def wave_table(longitudes, count):
    column = jnp.arange(longitudes, dtype=jnp.int32)
    numbers = jnp.arange(count, dtype=jnp.int32)
    phase = column[:, None] * numbers[None, :] % longitudes
    angles = phase.astype(jnp.float32) * (2.0 * jnp.pi / longitudes)
    scale = jnp.float32(longitudes) ** (-0.5)
    return jnp.concatenate([jnp.cos(angles), -jnp.sin(angles)], axis=1) * scale


def fold(data):
    half = data.shape[2] // 2
    north = data[:, :, :half]
    south = data[:, :, half:][:, :, ::-1]
    return (north + south, north - south)


def by_parity(even_part, odd_part):
    depth_index = jnp.arange(even_part.shape[1], dtype=jnp.int32)
    keep = (depth_index % 2 == 0)[None, :, None, None]
    return jnp.where(keep, even_part, odd_part)


def analyse(north_table, even, odd):
    highest = lax.Precision.HIGHEST
    even_part = jnp.einsum("skt,cstl->skcl", north_table, even, precision=highest)
    odd_part = jnp.einsum("skt,cstl->skcl", north_table, odd, precision=highest)
    return by_parity(even_part, odd_part)


def synthesise(north_table, coeffs):
    highest = lax.Precision.HIGHEST
    depth = north_table.shape[1]
    depth_index = jnp.arange(depth, dtype=jnp.int32)
    even_mask = (depth_index % 2 == 0).astype(jnp.float32)[None, :, None, None]
    even_coeffs = coeffs * even_mask
    odd_coeffs = coeffs - even_coeffs
    first = jnp.einsum("skt,skcl->cstl", north_table, even_coeffs, precision=highest)
    second = jnp.einsum("skt,skcl->cstl", north_table, odd_coeffs, precision=highest)
    north = first + second
    south = (first - second)[:, :, ::-1]
    return jnp.concatenate([north, south], axis=2)


def couple(analysed, state, wavenumbers, to_modes, from_modes, rates):
    highest = lax.Precision.HIGHEST
    depth = analysed.shape[1]
    depth_index = jnp.arange(depth, dtype=jnp.int32)
    valid = (depth_index[None, :] < depth - wavenumbers[:, None]).astype(jnp.float32)
    total = (analysed + state) * valid[:, :, None, None]
    degree = (wavenumbers[:, None] + depth_index[None, :]).astype(jnp.float32)
    helm = degree * (degree + 1.0) / (depth * (depth - 1.0))
    modes = jnp.einsum("skcl,pl->skcp", total, to_modes, precision=highest)
    scaled = modes / (1.0 + helm[:, :, None, None] * rates)
    return jnp.einsum("skcp,lp->skcl", scaled, from_modes, precision=highest)


def shards(
    grid_adjoint,
    trajectory,
    legendre_north,
    slot_wavenumber,
    spectral_state,
    to_modes,
    from_modes,
    rates,
):
    highest = lax.Precision.HIGHEST
    lat_rows, level_rows, longitudes = grid_adjoint.shape
    width = slot_wavenumber.shape[0]
    slot_rows = legendre_north.shape[0]
    bands = lax.axis_size("band")
    levels_count = lax.axis_size("lev")
    band_at = lax.axis_index("band")
    level_at = lax.axis_index("lev")
    table = wave_table(longitudes, width)
    counting = jnp.arange(width, dtype=jnp.int32)
    inverse = jnp.zeros((width,), jnp.int32).at[slot_wavenumber].set(counting)
    forced = grid_adjoint * (1.0 + trajectory)
    flat = forced.reshape(lat_rows * level_rows, longitudes)
    natural = lax.dot_general(
        table, flat, (((0,), (1,)), ((), ())), precision=highest, preferred_element_type=jnp.float32
    )
    natural = natural.reshape(2, width, lat_rows * level_rows)
    fourier = jnp.take(natural, slot_wavenumber, axis=1).reshape(2, width, lat_rows, level_rows)
    own_start = (band_at * levels_count + level_at) * slot_rows
    own_waves = lax.dynamic_slice_in_dim(slot_wavenumber, own_start, slot_rows)
    gathered = lax.all_to_all(
        lax.all_to_all(fourier, "band", split_axis=1, concat_axis=2, tiled=True),
        "lev",
        split_axis=1,
        concat_axis=3,
        tiled=True,
    )
    even, odd = fold(gathered)
    analysed = analyse(legendre_north, even, odd)
    spectral_out = couple(analysed, spectral_state, own_waves, to_modes, from_modes, rates)
    synthesised = synthesise(legendre_north, spectral_out)
    returned = lax.all_to_all(
        lax.all_to_all(synthesised, "band", split_axis=2, concat_axis=1, tiled=True),
        "lev",
        split_axis=3,
        concat_axis=1,
        tiled=True,
    )
    level_part = counting // (bands * slot_rows)
    band_part = counting // slot_rows % bands
    within = counting % slot_rows
    source_slot = band_part * (levels_count * slot_rows) + level_part * slot_rows + within
    arrival_of_slot = jnp.zeros((width,), jnp.int32).at[source_slot].set(counting)
    pick = jnp.take(arrival_of_slot, inverse, axis=0)
    ordered = jnp.take(returned.reshape(2, width, lat_rows * level_rows), pick, axis=1)
    coeff_rows = ordered.reshape(2 * width, lat_rows * level_rows)
    grid_out = lax.dot_general(
        coeff_rows,
        table,
        (((0,), (1,)), ((), ())),
        precision=highest,
        preferred_element_type=jnp.float32,
    )
    return (spectral_out, grid_out.reshape(lat_rows, level_rows, longitudes))


def solution(mesh):
    return jax.shard_map(
        shards,
        mesh=mesh,
        in_specs=(
            P("band", "lev", None),
            P("band", "lev", None),
            P(("band", "lev"), None, None),
            P(),
            P(("band", "lev"), None, None, None),
            P(),
            P(),
            P(),
        ),
        out_specs=(P(("band", "lev"), None, None, None), P("band", "lev", None)),
        check_vma=False,
    )
```

profile of v0, /device:TPU:0, one launch (start us, length us, event | category | flops | bytes accessed | tf_op | source)
XLA Modules:
  0.0 1142.8 jit_solution(12280588452169938446)
XLA Ops:
  0.7 16.5 %sine_negate_fusion = (f32[2048,512]{1,0:T(8,128)S(1)}, f32[2048,512]{1,0:T(8,128)S(1)}) fusion(), kind=kLoop, calls=%fused_computation.41 | loop fusion | flops 15728640 | bytes 8388608 | tf_op jit(solution)/shard_map/neg | solution.py:13
  25.3 9.2 copy.79
  34.5 11.7 %add_multiply_fusion = f32[128,16,2048]{2,1,0:T(8,128)S(1)} fusion(f32[128,16,2048]{2,1,0:T(8,128)} %param.10, f32[128,16,2048]{2,1,0:T(8,128)} %param.11), kind=kLoop, calls=%fused_computation.13 | loop fusion | flops 8388608 | bytes 50331648 | tf_op jit(solution)/shard_map/mul | solution.py:84
  46.2 67.1 %fusion.57 = f32[2,512,2048]{2,1,0:T(8,128)} fusion(f32[2,512,2048]{2,1,0:T(8,128)} %bitcast.91, f32[2048,2048,1]{1,0,2:T(8,128)S(1)} %bitcast.89), kind=kOutput, calls=%fused_computation.99 | convolution fusion | flops 51539607552 | bytes 33554432 | tf_op jit(solution)/shard_map/dot_general | solution.py:86
  113.3 15.4 %copy.80 = f32[2,512,2048]{2,0,1:T(2,128)} copy(f32[2,512,2048]{2,1,0:T(8,128)} %fusion.57) | data formatting | bytes 16777216 | tf_op jit(solution)/shard_map/dot_general | solution.py:86
  128.7 22.7 %gather_fusion.1 = f32[512,2,2048]{2,1,0:T(2,128)} fusion(f32[2,512,2048]{2,0,1:T(2,128)} %copy.80, s32[1024]{0:T(1024)S(1)} %pad_clamp_fusion.2), kind=kCustom, calls=%fused_computation.clone | custom fusion | bytes 16779264 | tf_op jit(solution)/shard_map/jit(_take)/gather | solution.py:90
  151.4 8.5 select_bitcast_fusion.1
  159.9 13.1 %copy.81 = f32[2,512,2048]{1,2,0:T(8,128)} copy(f32[2,512,2048]{2,0,1:T(2,128)} %select_bitcast_fusion.1) | data formatting | bytes 16777216 | tf_op jit(solution)/shard_map/jit(_take)/select_n | solution.py:90
  173.0 10.8 copy.82
  183.8 190.4 %all_to_all.69 = f32[2,512,128,16]{2,3,0,1:T(8,128)S(1)} all-to-all(f32[2,512,128,16]{2,3,0,1:T(8,128)} %copy.82), channel_id=1, replica_groups=mesh['band'=8,'lev'=4] {'band'}, dimensions={1} | all-to-all | bytes 16777216 | tf_op jit(solution)/shard_map/all_to_all | solution.py:94
  386.7 91.2 %all-to-all-done.1 = f32[2,64,1024,16]{2,3,0,1:T(8,128)} async-done(((f32[2,64,1024,16]{2,3,0,1:T(8,128)}), f32[2,64,1024,16]{2,3,0,1:T(8,128)}, u32[]{:S(2)}, u32[]{:S(2)}) %all-to-all-start.1) | async-done | bytes 8388640 | tf_op jit(solution)/shard_map/all_to_all | solution.py:93
  500.0 21.0 %fusion.4 = f32[16,2,64,512]{3,2,1,0:T(8,128)S(1)} fusion(f32[16,512,512]{2,1,0:T(8,128)} %param.12, f32[2,16,512,64]{2,3,1,0:T(8,128)S(1)} %get-tuple-element.19), kind=kOutput, calls=%fused_computation.9 | convolution fusion | flops 6442450944 | bytes 25165824 | tf_op jit(solution)/shard_map/skt,cstl->skcl/dot_general | solution.py:32
  521.0 21.6 %fusion.6 = f32[16,2,64,512]{3,2,1,0:T(8,128)S(1)} fusion(f32[16,512,512]{2,1,0:T(8,128)} %param.12, f32[2,16,512,64]{2,3,1,0:T(8,128)S(1)} %get-tuple-element.20), kind=kOutput, calls=%fused_computation.11 | convolution fusion | flops 6442450944 | bytes 25165824 | tf_op jit(solution)/shard_map/skt,cstl->skcl/dot_general | solution.py:31
  542.7 7.9 fusion.16
  555.6 16.0 %fusion = f32[16,2,64,512]{3,2,1,0:T(8,128)} fusion(f32[16,512,512]{2,1,0:T(8,128)} %param.12, f32[16,512,2,64]{1,3,2,0:T(8,128)S(1)} %fusion.20, f32[512]{0:T(512)S(1)} %fusion.50), kind=kOutput, calls=%fused_computation.5 | convolution fusion | flops 6444548096 | bytes 25167872 | tf_op jit(solution)/shard_map/skt,skcl->cstl/dot_general | solution.py:44
  571.7 15.8 %add_bitcast_fusion = (f32[2,16,512,64]{2,3,0,1:T(8,128)}, f32[2,16,512,64]{2,3,0,1:T(8,128)}) fusion(f32[16,2,64,512]{3,2,1,0:T(8,128)} %fusion, f32[16,512,512]{2,1,0:T(8,128)} %param.12, f32[16,512,2,64]{1,3,2,0:T(8,128)S(1)} %fusion.20, f32[512]{0:T(512)S(1)} %fusion.50), kind=kOutput, calls=%fused_computation.36 | convolution fusion | flops 6445596672 | bytes 33556480 | tf_op jit(solution)/shard_map/skt,skcl->cstl/dot_general | solution.py:43
  587.5 7.4 rev.7
  595.0 8.1 pad_maximum_fusion
  603.1 23.1 %copy.90 = f32[2,16,1024,64]{3,0,1,2:T(2,128)} copy(f32[2,16,1024,64]{2,3,0,1:T(8,128)} %pad_maximum_fusion) | data formatting | bytes 16777216 | tf_op jit(solution)/shard_map/concatenate | solution.py:47
  626.2 20.1 %reshape.290 = f32[8,1,262144]{2,1,0:T(1,128)} reshape(f32[1024,16,2,64]{3,2,1,0:T(2,128)} %bitcast.80) | data formatting | bytes 16777216
  646.3 188.7 %all_to_all.70 = f32[8,1,262144]{2,1,0:T(1,128)} all-to-all(f32[8,1,262144]{2,1,0:T(1,128)} %reshape.290), channel_id=1, replica_groups=mesh['band'=8,'lev'=4] {'band'}, dimensions={0} | all-to-all | bytes 16777216 | tf_op jit(solution)/shard_map/all_to_all | solution.py:105
  835.6 26.7 %reduce = f32[8,262144]{1,0:T(8,128)} reduce(f32[8,1,262144]{2,1,0:T(1,128)} %all_to_all.70, f32[]{:T(128)} %broadcast.326), dimensions={1}, to_apply=%all_to_all.58.reduce_sub_computation | reduce | bytes 16777220 | tf_op jit(solution)/shard_map/all_to_all | solution.py:105
  862.2 25.7 %reshape.291 = f32[1024,16,2,64]{3,2,1,0:T(2,128)} reshape(f32[8,262144]{1,0:T(8,128)} %reduce) | data formatting | bytes 16777216
  887.9 17.4 %copy.111 = f32[2,16,8,128,64]{3,1,2,0,4:T(8,128)} copy(f32[2,16,8,128,64]{4,0,1,3,2:T(2,128)} %bitcast.81) | data formatting | bytes 16777216 | tf_op jit(solution)/shard_map/all_to_all | solution.py:105
  919.4 84.7 %all-to-all-done.3 = f32[2,128,128,64]{2,1,0,3:T(8,128)} async-done(((f32[2,128,128,64]{2,1,0,3:T(8,128)}), f32[2,128,128,64]{2,1,0,3:T(8,128)}, u32[]{:S(2)}, u32[]{:S(2)}) %all-to-all-start.3) | async-done | bytes 8388640 | tf_op jit(solution)/shard_map/all_to_all | solution.py:104
  1004.1 10.3 copy.95
  1014.3 10.3 reshape.230
  1024.7 13.3 %copy.96 = f32[2,512,2048]{2,0,1:T(2,128)} copy(f32[2,512,2048]{1,2,0:T(8,128)} %reshape.230) | data formatting | bytes 16777216 | tf_op jit(solution)/shard_map/reshape | solution.py:117
  1037.9 22.7 %gather_fusion.2 = f32[512,2,2048]{2,1,0:T(2,128)} fusion(f32[2,512,2048]{2,0,1:T(2,128)} %copy.96, s32[1024]{0:T(1024)S(1)} %pad_clamp_fusion), kind=kCustom, calls=%fused_computation.1.clone | custom fusion | bytes 16779264 | tf_op jit(solution)/shard_map/jit(_take)/gather | solution.py:117
  1067.0 8.3 copy.97
  1075.3 9.3 copy.98
  1084.5 58.0 %fusion.8 = f32[128,16,2048]{2,1,0:T(8,128)} fusion(f32[128,16,1024]{2,1,0:T(8,128)} %bitcast.90, f32[2048,512]{1,0:T(8,128)} %copy-done.4, f32[2048,512]{1,0:T(8,128)} %copy-done.5), kind=kOutput, calls=%fused_computation.17 | convolution fusion | flops 51543801856 | bytes 33554432 | tf_op jit(solution)/shard_map/dot_general | solution.py:119
  (50 shorter events, 68.7 us)
Async XLA Ops:
  0.6 542.0 %copy-start = (f32[64,64]{1,0:T(8,128)S(1)}, f32[64,64]{1,0:T(8,128)}, u32[]{:S(2)}) copy-start(f32[64,64]{1,0:T(8,128)} %param.15) | copy-start | bytes 49156
  0.6 16.5 %copy-start.7 = (s32[512]{0:T(512)S(1)}, s32[512]{0:T(512)}, u32[]{:S(2)}) copy-start(s32[512]{0:T(512)} %param.13) | copy-start | bytes 6148
  17.2 1.9 copy-start.4
  17.2 3.2 copy-start.5
  378.7 6.2 copy-start.8
  378.7 99.1 %all-to-all-start.1 = ((f32[2,64,1024,16]{2,3,0,1:T(8,128)}), f32[2,64,1024,16]{2,3,0,1:T(8,128)}, u32[]{:S(2)}, u32[]{:S(2)}) async-start(f32[2,64,1024,16]{2,3,0,1:T(8,128)} %bitcast.83), calls=%async_computation.1 | async-start | bytes 16777216 | tf_op jit(solution)/shard_map/all_to_all | solution.py:93
  482.0 3.4 copy-start.2
  542.7 7.9 copy-start.6
  542.7 7.9 copy-start.9
  555.6 16.1 %copy-start.3 = (f32[16,512,2,64]{1,3,2,0:T(8,128)}, f32[16,512,2,64]{1,3,2,0:T(8,128)S(1)}, u32[]{:S(2)}) copy-start(f32[16,512,2,64]{1,3,2,0:T(8,128)S(1)} %fusion.20) | copy-start | bytes 12582916
  905.3 98.8 %all-to-all-start.3 = ((f32[2,128,128,64]{2,1,0,3:T(8,128)}), f32[2,128,128,64]{2,1,0,3:T(8,128)}, u32[]{:S(2)}, u32[]{:S(2)}) async-start(f32[2,128,128,64]{2,1,0,3:T(8,128)} %bitcast.82), calls=%async_computation.3 | async-start | bytes 16777216 | tf_op jit(solution)/shard_map/all_to_all | solution.py:104
  1084.5 58.0 %copy-start.1 = (f32[64,64]{1,0:T(8,128)S(1)}, f32[64,64]{1,0:T(8,128)}, u32[]{:S(2)}) copy-start(f32[64,64]{1,0:T(8,128)} %param.15) | copy-start | bytes 49156
where the time goes:
time: 1150 us; the launch traced here: 1140 us
  blocking collectives  379 us (33%)
  local copies, waits for them, and re-layouts  273 us (24%)
  matrix products  213 us (19%)
  waiting for transfers between devices  176 us (15%)
  other arithmetic  89.4 us (8%)
  starting transfers between devices  11.6 us (1%)
    all_to_all x1, blocking collectives, shards(): lax.all_to_all(fourier, 'band', split_axis=1, concat_axis=2, tiled=True)  190 us
    all_to_all x1, blocking collectives, shards(): lax.all_to_all(synthesised, 'band', split_axis=2, concat_axis=1, tiled=True)  189 us
    all_to_all x1, waiting for transfers between devices, shards(): lax.all_to_all(lax.all_to_all(fourier, 'band', split_axis=1, concat_axis=...  91.2 us
    all_to_all x1, waiting for transfers between devices, shards(): lax.all_to_all(lax.all_to_all(synthesised, 'band', split_axis=2, concat_a...  84.7 us
    dot_general x1, matrix products, shards(): lax.dot_general(table, flat, (((0,), (1,)), ((), ())), precision=highest,...  67.1 us
    dot_general x1, matrix products, shards(): lax.dot_general(coeff_rows, table, (((0,), (1,)), ((), ())), precision=hi...  58 us
    unnamed x22, local copies, waits for them, and re-layouts  52.5 us
    all_to_all x1, other arithmetic, shards(): lax.all_to_all(synthesised, 'band', split_axis=2, concat_axis=1, tiled=True)  26.7 us
  transfers between devices with their start and end apart: 2, of which 2 were waited for; matrix products, arithmetic and copies ran while one was open for 1% of the time, Pallas kernels for 0%

commit v1 on v0

v1 whole, which is shorter than its diff:
```python
import jax
import jax.numpy as jnp
from jax import lax
from jax.sharding import PartitionSpec as P

PRECISION = lax.Precision.HIGH


def angle_parts(steps, waves, longitudes):
    phase = waves[:, None] * steps[None, :] % longitudes
    angles = phase.astype(jnp.float32) * (2.0 * jnp.pi / longitudes)
    return jnp.cos(angles), jnp.sin(angles)


def wave_rows(longitudes, waves, devices):
    fine = min(128, longitudes)
    coarse = longitudes // fine
    scale = jnp.float32(longitudes) ** (-0.5)
    cos_a, sin_a = angle_parts(jnp.arange(coarse, dtype=jnp.int32) * fine, waves, longitudes)
    cos_b, sin_b = angle_parts(jnp.arange(fine, dtype=jnp.int32), waves, longitudes)
    cos_a, sin_a, cos_b, sin_b = lax.optimization_barrier(
        (cos_a * scale, sin_a * scale, cos_b, sin_b)
    )
    cos_at = [cos_a[:, i : i + 1] * cos_b - sin_a[:, i : i + 1] * sin_b for i in range(coarse)]
    sin_at = [-sin_a[:, i : i + 1] * cos_b - cos_a[:, i : i + 1] * sin_b for i in range(coarse)]
    cosine = jnp.concatenate(cos_at, axis=1).reshape(devices, -1, longitudes)
    negsine = jnp.concatenate(sin_at, axis=1).reshape(devices, -1, longitudes)
    return jnp.stack([cosine, negsine], axis=1).reshape(-1, longitudes)


def exchange(data):
    return lax.all_to_all(data, ("band", "lev"), split_axis=0, concat_axis=0, tiled=True)


def shards(
    grid_adjoint,
    trajectory,
    legendre_north,
    slot_wavenumber,
    spectral_state,
    to_modes,
    from_modes,
    rates,
):
    lats, levels, longitudes = grid_adjoint.shape
    slots, depth, half = legendre_north.shape
    bands = lax.axis_size("band")
    parts = lax.axis_size("lev")
    devices = bands * parts
    every = parts * levels
    me = lax.axis_index("band") * parts + lax.axis_index("lev")
    own_waves = lax.dynamic_slice_in_dim(slot_wavenumber, me * slots, slots)
    table = wave_rows(longitudes, slot_wavenumber, devices)
    even_k = jnp.arange(depth, dtype=jnp.int32) % 2 == 0

    forced = grid_adjoint * (1.0 + trajectory)
    rows = jnp.swapaxes(forced, 0, 1).reshape(levels * lats, longitudes)
    fourier = lax.dot_general(
        table, rows, (((1,), (1,)), ((), ())), precision=PRECISION, preferred_element_type=jnp.float32
    )
    arrived = exchange(fourier.reshape(devices, 2 * slots, levels * lats))
    arrived = arrived.reshape(bands, parts, 2, slots, levels, lats)
    arrived = arrived.transpose(3, 2, 1, 4, 0, 5).reshape(slots, 2 * every, bands * lats)
    north = arrived[:, :, :half]
    south = arrived[:, :, half:][:, :, ::-1]
    folded = jnp.concatenate([north + south, north - south], axis=1)
    both = lax.dot_general(
        folded, legendre_north, (((2,), (2,)), ((0,), (0,))), precision=PRECISION,
        preferred_element_type=jnp.float32,
    )
    analysed = jnp.where(even_k, both[:, : 2 * every], both[:, 2 * every :])
    analysed = analysed.reshape(slots, 2, every, depth)

    state = spectral_state.transpose(0, 2, 3, 1)
    depth_index = jnp.arange(depth, dtype=jnp.int32)
    valid = (depth_index[None, :] < depth - own_waves[:, None]).astype(jnp.float32)
    total = (analysed + state) * valid[:, None, None, :]
    degree = (own_waves[:, None] + depth_index[None, :]).astype(jnp.float32)
    helm = degree * (degree + 1.0) / (depth * (depth - 1.0))
    modes = jnp.einsum("sclk,pl->scpk", total, to_modes, precision=PRECISION)
    scaled = modes / (1.0 + helm[:, None, None, :] * rates[None, None, :, None])
    spectral = jnp.einsum("scpk,lp->sclk", scaled, from_modes, precision=PRECISION)

    coeffs = spectral.reshape(slots, 2 * every, depth)
    split = jnp.concatenate(
        [jnp.where(even_k, coeffs, 0.0), jnp.where(even_k, 0.0, coeffs)], axis=1
    )
    halves = lax.dot_general(
        split, legendre_north, (((2,), (1,)), ((0,), (0,))), precision=PRECISION,
        preferred_element_type=jnp.float32,
    )
    first = halves[:, : 2 * every]
    second = halves[:, 2 * every :]
    whole = jnp.concatenate([first + second, (first - second)[:, :, ::-1]], axis=2)
    whole = whole.reshape(slots, 2, parts, levels, bands, lats).transpose(4, 2, 1, 0, 3, 5)
    returned = exchange(whole.reshape(devices, 2 * slots, levels * lats))
    grid = lax.dot_general(
        returned.reshape(devices * 2 * slots, levels, lats),
        table,
        (((0,), (0,)), ((), ())),
        precision=PRECISION,
        preferred_element_type=jnp.float32,
    )
    return spectral.transpose(0, 3, 1, 2), jnp.swapaxes(grid, 0, 1)


def solution(mesh):
    return jax.shard_map(
        shards,
        mesh=mesh,
        in_specs=(
            P("band", "lev", None),
            P("band", "lev", None),
            P(("band", "lev"), None, None),
            P(),
            P(("band", "lev"), None, None, None),
            P(),
            P(),
            P(),
        ),
        out_specs=(P(("band", "lev"), None, None, None), P("band", "lev", None)),
        check_vma=False,
    )
```

time: 1150 us -> 717 us (0.62)
  blocking collectives: 379 us -> 187 us
  local copies, waits for them, and re-layouts: 273 us -> 146 us
  matrix products: 213 us -> 104 us
  other arithmetic: 89.4 us -> 72.7 us
    all_to_all x2 -> x1, blocking collectives: 379 us -> 187 us  [exchange(): lax.all_to_all(data, ('band', 'lev'), split_axis=0, concat_axis=0, tiled=...]
    dot_general x8 -> x6, matrix products: 213 us -> 104 us  [the longest x1 35.7 us: shards(): lax.dot_general(returned.reshape(devices * 2 * slots, levels, lats), tabl...]
    rev x2, local copies, waits for them, and re-layouts: 14.8 us -> 68.4 us  [the longest x1 34.2 us: shards(): (first - second)[:, :, ::-1]]
    gather x3 -> x0, local copies, waits for them, and re-layouts: 48.9 us -> none  [the longest x1 22.7 us: shards(): jnp.take(returned.reshape(2, width, lat_rows * level_rows), pick, axis=1)]
    all_to_all x5 -> x0, local copies, waits for them, and re-layouts: 37 us -> none  [the longest x2 17.9 us: shards(): lax.all_to_all(synthesised, 'band', split_axis=2, concat_axis=1, tiled=True)]
    dot_general x3 -> x0, local copies, waits for them, and re-layouts: 33.9 us -> none  [the longest x2 24.6 us: shards(): lax.dot_general(table, flat, (((0,), (1,)), ((), ())), precision=highest,...]
    all_to_all x1 -> x0, other arithmetic: 26.7 us -> none  [shards(): lax.all_to_all(synthesised, 'band', split_axis=2, concat_axis=1, tiled=True)]
    concatenate x1 -> x0, local copies, waits for them, and re-layouts: 23.1 us -> none  [synthesise(): return jnp.concatenate([north, south], axis=2)]
  transfers between devices with their start and end apart: 2 -> 1, of which waited for: 2 -> 1; matrix products, arithmetic and copies ran while one was open for 1% -> 0% of each run, Pallas kernels for 0% -> 0%
where the time goes in v1:
time: 717 us; the launch traced here: 703 us
  blocking collectives  187 us (26%)
  waiting for transfers between devices  185 us (26%)
  local copies, waits for them, and re-layouts  146 us (20%)
  matrix products  104 us (15%)
  other arithmetic  72.7 us (10%)
  starting transfers between devices  7.86 us (1%)
    all_to_all x1, blocking collectives, exchange(): lax.all_to_all(data, ('band', 'lev'), split_axis=0, concat_axis=0, tiled=...  187 us
    all_to_all x1, waiting for transfers between devices, exchange(): lax.all_to_all(data, ('band', 'lev'), split_axis=0, concat_axis=0, tiled=...  185 us
    unnamed x26, local copies, waits for them, and re-layouts  38.1 us
    dot_general x1, matrix products, shards(): lax.dot_general(returned.reshape(devices * 2 * slots, levels, lats), tabl...  35.7 us
    rev x1, local copies, waits for them, and re-layouts, shards(): (first - second)[:, :, ::-1]  34.2 us
    rev x1, local copies, waits for them, and re-layouts, shards(): south = arrived[:, :, half:][:, :, ::-1]  34.2 us
    dot_general x1, matrix products, shards(): lax.dot_general(table, rows, (((1,), (1,)), ((), ())), precision=PRECISIO...  33.2 us
    mul x1, other arithmetic, shards(): forced = grid_adjoint * (1.0 + trajectory)  27.3 us
  transfers between devices with their start and end apart: 1, of which 1 were waited for; matrix products, arithmetic and copies ran while one was open for 0% of the time, Pallas kernels for 0%

profile of v1, /device:TPU:0, one launch (start us, length us, event | category | flops | bytes accessed | tf_op | source)
XLA Modules:
  0.0 703.2 jit_solution(9347582182654225411)
XLA Ops:
  0.7 1.8 fusion.25
  2.4 0.9 sine_multiply_fusion
  7.9 2.0 copy-done.2
  9.9 6.6 pad_maximum_fusion
  16.5 27.3 %copy_multiply_fusion = f32[128,16,2048]{2,0,1:T(8,128)} fusion(f32[128,16,2048]{2,1,0:T(8,128)S(1)} %bitcast.117, f32[128,16,2048]{2,1,0:T(8,128)} %param.9), kind=kLoop, calls=%fused_computation | loop fusion | flops 8388608 | bytes 50331648 | tf_op jit(solution)/shard_map/mul | solution.py:56
  43.9 33.2 %fusion.43 = f32[32,32,2048]{2,1,0:T(8,128)} fusion(f32[32,32,2048]{2,1,0:T(8,128)} %bitcast.120, f32[2048,2048,1]{1,0,2:T(8,128)} %bitcast.118), kind=kOutput, calls=%fused_computation.119 | convolution fusion | flops 25769803776 | bytes 33554432 | tf_op jit(solution)/shard_map/dot_general | solution.py:58
  77.0 7.9 %all-to-all-start = ((f32[32,32,2048]{2,1,0:T(8,128)}), f32[32,32,2048]{2,1,0:T(8,128)}, u32[]{:S(2)}, u32[]{:S(2)}) async-start(f32[32,32,2048]{2,1,0:T(8,128)} %fusion.43), calls=%async_computation | async-start | bytes 16777216 | tf_op jit(solution)/shard_map/all_to_all | solution.py:32
  84.9 0.8 broadcast_subtract_fusion
  85.9 0.3 multiply_add_fusion
  86.2 184.6 %all-to-all-done = f32[32,32,2048]{2,1,0:T(8,128)} async-done(((f32[32,32,2048]{2,1,0:T(8,128)}), f32[32,32,2048]{2,1,0:T(8,128)}, u32[]{:S(2)}, u32[]{:S(2)}) %all-to-all-start) | async-done | bytes 8388640 | tf_op jit(solution)/shard_map/all_to_all | solution.py:32
  270.8 5.4 copy.20
  276.2 8.3 %copy.14 = f32[16,2,4,16,8,128]{5,4,3,2,1,0:T(8,128)} copy(f32[16,2,4,16,8,128]{5,3,0,1,2,4:T(8,128)S(1)} %bitcast.112) | data formatting | bytes 16777216 | tf_op jit(solution)/shard_map/transpose | solution.py:63
  284.4 9.2 %reshape.90 = f32[16,128,1024]{2,1,0:T(8,128)} reshape(f32[16,2,4,16,8,128]{5,4,3,2,1,0:T(8,128)} %copy.14) | data formatting | bytes 16777216 | tf_op jit(solution)/shard_map/reshape | solution.py:63
  293.7 4.8 slice.185
  298.5 34.2 %rev.6 = f32[16,128,512]{2,1,0:T(8,128)} reverse(f32[16,128,512]{2,1,0:T(8,128)} %slice.185), dimensions={2} | reverse | bytes 8388608 | tf_op jit(solution)/shard_map/rev | solution.py:65
  332.7 8.4 %slice_add_fusion.1 = (f32[16,128,512]{2,1,0:T(8,128)}, f32[16,128,512]{2,1,0:T(8,128)}) fusion(f32[16,128,512]{2,1,0:T(8,128)} %rev.6, f32[16,128,1024]{2,1,0:T(8,128)} %reshape.90), kind=kLoop, calls=%fused_computation.27 | loop fusion | flops 2097152 | bytes 16777216 | tf_op jit(solution)/shard_map/add | solution.py:66
  341.1 14.3 %fusion = f32[16,256,512]{2,1,0:T(8,128)} fusion(f32[16,512,512]{2,1,0:T(8,128)} %param.10, f32[16,128,512]{2,1,0:T(8,128)} %get-tuple-element.17, f32[16,128,512]{2,1,0:T(8,128)} %get-tuple-element.16), kind=kOutput, calls=%fused_computation.3 | convolution fusion | flops 6444548096 | bytes 33554432 | tf_op jit(solution)/shard_map/dot_general | solution.py:67
  355.4 4.6 slice_select_fusion
  360.1 2.9 fusion.15
  363.1 2.5 fusion.13
  365.6 4.6 bitcast_select_fusion.1
  370.2 15.1 %fusion.4 = f32[16,256,512]{2,1,0:T(8,128)} fusion(f32[16,512,512]{2,1,0:T(8,128)} %param.10, f32[16,128,512]{2,1,0:T(8,128)} %get-tuple-element.21, f32[16,128,512]{2,1,0:T(8,128)} %get-tuple-element.20), kind=kOutput, calls=%fused_computation.7 | convolution fusion | flops 6444548096 | bytes 33554432 | tf_op jit(solution)/shard_map/dot_general | solution.py:88
  385.2 8.3 %slice_add_fusion = (f32[16,128,512]{2,1,0:T(8,128)}, f32[16,128,512]{2,1,0:T(8,128)}) fusion(f32[16,256,512]{2,1,0:T(8,128)} %fusion.4), kind=kLoop, calls=%fused_computation.25 | loop fusion | flops 2097152 | bytes 16777216 | tf_op jit(solution)/shard_map/add | solution.py:94
  393.6 34.2 %rev.7 = f32[16,128,512]{2,1,0:T(8,128)} reverse(f32[16,128,512]{2,1,0:T(8,128)} %get-tuple-element.19), dimensions={2} | reverse | bytes 8388608 | tf_op jit(solution)/shard_map/rev | solution.py:94
  427.8 4.5 pad_maximum_fusion.1
  432.3 5.5 copy.21
  437.8 8.3 %copy.32 = f32[16,2,4,16,8,128]{5,3,0,1,2,4:T(8,128)} copy(f32[16,2,4,16,8,128]{5,4,3,2,1,0:T(8,128)} %bitcast.113) | data formatting | bytes 16777216 | tf_op jit(solution)/shard_map/reshape | solution.py:95
  446.1 9.2 %reshape.94 = f32[32,32,2048]{2,1,0:T(8,128)} reshape(f32[8,4,2,16,16,128]{5,4,3,2,1,0:T(8,128)} %bitcast.114) | data formatting | bytes 16777216 | tf_op jit(solution)/shard_map/reshape | solution.py:96
  455.3 186.6 %all_to_all.10 = f32[32,32,2048]{2,1,0:T(8,128)S(1)} all-to-all(f32[32,32,2048]{2,1,0:T(8,128)} %reshape.94), channel_id=1, replica_groups=mesh['band'=8,'lev'=4] {'band','lev'}, dimensions={0} | all-to-all | bytes 16777216 | tf_op jit(solution)/shard_map/all_to_all | solution.py:32
  641.9 5.4 copy.22
  647.2 35.7 %fusion.10 = f32[128,16,2048]{2,0,1:T(8,128)S(1)} fusion(f32[1024,2048,1]{1,0,2:T(8,128)} %bitcast.121, f32[1024,16,128]{2,1,0:T(8,128)} %bitcast.122), kind=kOutput, calls=%fused_computation.15 | convolution fusion | flops 25769803776 | bytes 33554432 | tf_op jit(solution)/shard_map/dot_general | solution.py:97
  682.9 19.8 %copy.17 = f32[128,16,2048]{2,1,0:T(8,128)} copy(f32[128,16,2048]{2,0,1:T(8,128)S(1)} %fusion.10) | data formatting | bytes 33554432
  (45 shorter events, 4.6 us)
Async XLA Ops:
  0.6 359.5 %copy-start = (f32[64,64]{1,0:T(8,128)S(1)}, f32[64,64]{1,0:T(8,128)}, u32[]{:S(2)}) copy-start(f32[64,64]{1,0:T(8,128)} %param.13) | copy-start | bytes 49156
  4.3 12.2 %slice-start = ((s8[16777216]{0:T(1024)(128)(4,1)}), s8[4194304]{0:T(1024)(128)(4,1)S(1)}, s32[]{:S(2)}) async-start(s8[16777216]{0:T(1024)(128)(4,1)} %bitcast.116), calls=%async_computation.2 | async-start | bytes 8388608
  6.2 10.3 %slice-start.1 = ((s8[16777216]{0:T(1024)(128)(4,1)}), s8[4194304]{0:T(1024)(128)(4,1)S(1)}, s32[]{:S(2)}) async-start(s8[16777216]{0:T(1024)(128)(4,1)} %bitcast.116), calls=%async_computation.3 | async-start | bytes 8388608
  7.9 2.0 copy-start.2
  9.9 6.6 slice-start.2
  9.9 6.6 slice-start.3
  77.0 8.8 %copy-start.5 = (f32[64]{0:T(128)S(1)}, f32[64]{0:T(128)}, u32[]{:S(2)}) copy-start(f32[64]{0:T(128)} %param.15) | copy-start | bytes 772
  77.0 193.7 %all-to-all-start = ((f32[32,32,2048]{2,1,0:T(8,128)}), f32[32,32,2048]{2,1,0:T(8,128)}, u32[]{:S(2)}, u32[]{:S(2)}) async-start(f32[32,32,2048]{2,1,0:T(8,128)} %fusion.43), calls=%async_computation | async-start | bytes 16777216 | tf_op jit(solution)/shard_map/all_to_all | solution.py:32
  355.4 4.7 copy-start.3
  360.1 2.9 copy-start.6
  365.6 4.6 copy-start.4
  682.9 19.8 %copy-start.1 = (f32[64,64]{1,0:T(8,128)S(1)}, f32[64,64]{1,0:T(8,128)}, u32[]{:S(2)}) copy-start(f32[64,64]{1,0:T(8,128)} %param.13) | copy-start | bytes 49156
